TPU v7x, 128 devices: a whole 4x4x4 slice. The times are simulated.
128 devices in a mesh: hx: 8 (over y, core), hy: 16 (over x, z).
Axes of the slice: x: 4, y: 4, z: 4, core: 2. Of those that a mesh axis runs over, the one named last changes fastest.
Arguments:
- embeddings: bfloat16 [65536, 768], P(('hx', 'hy')), may hold values from -60 to 60
- bucket: int32 [65536], P(('hx', 'hy')), may hold values from 0 to 255, as said below
Outputs:
- smoothed: bfloat16 [65536, 768], P(('hx', 'hy'))
Inputs may be any that keep to these rules, and one draw needn't show every extreme that they name: Every bucket holds at most 512 files and some bucket holds exactly 512; buckets may be empty. The files of each bucket, and of each owner's 2 buckets taken together, lie on the devices as evenly as can be (counts on two devices differ by at most one), so that no device holds more than 8 files of one owner's buckets, and some owner's buckets give exactly 8 to every device.
All inputs are finite; a program needn't handle non-finite values.
Results may differ from a plain program's by a relative error of at most 0.0042.
Values may be sent and summed in bfloat16 or wider, within the bound.
A program may use at most 64 MiB of HBM per device.

v0:
```python
import jax
import jax.numpy as jnp
from jax import lax
from jax.sharding import PartitionSpec as P

BPD = 2
CAP = 512


sharpness = 32.0
epsilon = 1e-06


def swapped(value, axis, apart):
    return lax.ppermute(value, axis, [(i, i ^ 1 << apart) for i in range(lax.axis_size(axis))])


def inverse_norm(rows):
    return 1.0 / jnp.sqrt(jnp.mean(jnp.square(rows.astype(jnp.float32)), axis=-1) + epsilon)


def rank_within(labels, groups):
    total_rows = labels.shape[0]
    block_rows = min(128, total_rows)
    block_count = total_rows // block_rows
    onehot = (labels[:, None] == jnp.arange(groups, dtype=jnp.int32)[None, :]).astype(jnp.bfloat16)
    stacked = onehot.reshape(block_count, block_rows, groups)
    lower = (jnp.arange(block_rows)[:, None] > jnp.arange(block_rows)[None, :]).astype(jnp.bfloat16)
    within = jnp.einsum("ij,bjn->bin", lower, stacked, preferred_element_type=jnp.float32)
    stacked_wide = stacked.astype(jnp.float32)
    totals = jnp.sum(stacked_wide, axis=1)
    offsets = jnp.cumsum(totals, axis=0) - totals
    before = within + offsets[:, None, :]
    rank_rows = jnp.sum(before * stacked_wide, axis=2).reshape(total_rows)
    return (rank_rows.astype(jnp.int32), jnp.sum(totals, axis=0).astype(jnp.int32))


def place_matrix(target, total):
    return (jnp.arange(total, dtype=jnp.int32)[:, None] == target[None, :]).astype(jnp.bfloat16)


def pick_back(matrix, values):
    return lax.dot_general(
        matrix, values, (((0,), (0,)), ((), ())), preferred_element_type=jnp.float32
    ).astype(jnp.bfloat16)


def body(embeddings, bucket):
    count_hx = lax.axis_size("hx")
    count_hy = lax.axis_size("hy")
    device_count = count_hx * count_hy
    feature_width = embeddings.shape[1]
    slot_size = BPD * CAP // device_count
    send_total = device_count * slot_size
    owner_dev = bucket // BPD
    local_slot = bucket % BPD
    slot_of, unused_counts = rank_within(owner_dev, device_count)
    send_match = place_matrix(owner_dev * slot_size + slot_of, send_total)
    send_flat = jnp.dot(send_match, embeddings, preferred_element_type=jnp.float32).astype(
        jnp.bfloat16
    )
    slot_tag = (local_slot + 1).astype(jnp.bfloat16)[:, None]
    send_tag = jnp.dot(send_match, slot_tag, preferred_element_type=jnp.float32)[:, 0]
    send_ids = send_tag.astype(jnp.int32) - 1
    got_rows, got_ids = (
        lax.all_to_all(
            send_flat.reshape(device_count, slot_size, feature_width),
            ("hx", "hy"),
            split_axis=0,
            concat_axis=0,
            tiled=True,
        ),
        lax.all_to_all(
            send_ids.reshape(device_count, slot_size),
            ("hx", "hy"),
            split_axis=0,
            concat_axis=0,
            tiled=True,
        ),
    )
    recv_total = device_count * slot_size
    recv_rows = got_rows.reshape(recv_total, feature_width)
    recv_ids = got_ids.reshape(recv_total)
    valid_row = recv_ids >= 0
    target_bucket = jnp.where(valid_row, recv_ids, BPD)
    rank_in, group_counts = rank_within(target_bucket, BPD + 1)
    own_counts = group_counts[:BPD]
    own_match = place_matrix(target_bucket * CAP + rank_in, BPD * CAP)
    own_blocks = (
        jnp.dot(own_match, recv_rows, preferred_element_type=jnp.float32)
        .astype(jnp.bfloat16)
        .reshape(BPD, CAP, feature_width)
    )
    hx_blocks, hx_counts = swapped((own_blocks, own_counts), "hx", count_hx.bit_length() - 2)
    hy_blocks, hy_counts = swapped((own_blocks, own_counts), "hy", count_hy.bit_length() - 2)
    own_inv = inverse_norm(own_blocks)
    hx_inv = inverse_norm(hx_blocks)
    hy_inv = inverse_norm(hy_blocks)
    query_block = min(512, CAP)
    column_index = jnp.arange(CAP, dtype=jnp.int32)
    factor = sharpness / feature_width
    out_list = []
    for which in range(BPD):
        other = which ^ 1
        key_sets = [
            (own_blocks[which], own_inv[which], own_counts[which], True),
            (own_blocks[other], own_inv[other], own_counts[other], False),
            (hx_blocks[which], hx_inv[which], hx_counts[which], False),
            (hy_blocks[which], hy_inv[which], hy_counts[which], False),
        ]
        query_rows = own_blocks[which, 0:query_block]
        query_inv = own_inv[which, 0:query_block]
        row_index = 0 + jnp.arange(query_block, dtype=jnp.int32)
        numerator = jnp.zeros((query_block, feature_width), jnp.float32)
        denominator = jnp.ones((query_block,), jnp.float32)
        for key_rows, key_inv, key_count, is_own in key_sets:
            products = lax.dot_general(
                query_rows, key_rows, (((1,), (1,)), ((), ())), preferred_element_type=jnp.float32
            )
            score = products * query_inv[:, None] * key_inv[None, :] * factor
            live = jnp.broadcast_to((column_index < key_count)[None, :], score.shape)
            if is_own:
                live = live & (row_index[:, None] != column_index[None, :])
            kernel = jnp.where(live, jnp.exp(score), jnp.float32(0.0))
            denominator = denominator + jnp.sum(kernel, axis=1)
            numerator = numerator + jnp.dot(
                kernel.astype(jnp.bfloat16), key_rows, preferred_element_type=jnp.float32
            )
        pieces = (numerator / denominator[:, None]).astype(jnp.bfloat16)
        out_list.append(pieces)
    out_flat = jnp.concatenate(out_list, axis=0)
    back_rows = pick_back(own_match, out_flat)
    home_rows = lax.all_to_all(
        back_rows.reshape(device_count, slot_size, feature_width),
        ("hx", "hy"),
        split_axis=0,
        concat_axis=0,
        tiled=True,
    )
    home_flat = home_rows.reshape(send_total, feature_width)
    return pick_back(send_match, home_flat)


def solution(mesh):
    return jax.shard_map(
        body,
        mesh=mesh,
        in_specs=(P(("hx", "hy"), None), P(("hx", "hy"))),
        out_specs=P(("hx", "hy"), None),
        check_vma=False,
    )
```

profile of v0, /device:TPU:1, one launch (start us, length us, event | category | flops | bytes accessed | tf_op | source)
XLA Modules:
  0.0 137.0 jit_solution(16078369452312610685)
XLA Ops:
  0.0 0.0 copy-start
  0.0 0.8 fusion.112
  0.8 0.1 convert_reduce_fusion
  0.9 0.2 fusion.52
  1.2 0.7 bitcast_add_fusion
  1.9 0.5 fusion.6
  2.3 0.7 sub.29
  3.0 11.5 %all-to-all-start = ((s32[128,1,8]{2,1,0:T(1,128)}), s32[128,1,8]{2,1,0:T(1,128)S(1)}, u32[]{:S(2)}, u32[]{:S(2)}) async-start(s32[128,1,8]{2,1,0:T(1,128)} %bitcast.5), calls=%async_computation | async-start | bytes 131072 | tf_op jit(solution)/shard_map/all_to_all | solution.py:73
  14.5 0.0 copy-done
  14.5 2.2 %fusion.15 = bf16[128,8,768]{2,1,0:T(8,128)(2,1)} fusion(bf16[512,768]{1,0:T(8,128)(2,1)S(1)} %copy-done, s32[512]{0:T(512)S(1)} %get-tuple-element.13), kind=kOutput, calls=%fused_computation.22 | convolution fusion | flops 806617088 | bytes 2361344 | tf_op jit(solution)/shard_map/dot_general | solution.py:59
  16.7 7.3 %all-to-all-done = s32[128,1,8]{2,1,0:T(1,128)S(1)} async-done(((s32[128,1,8]{2,1,0:T(1,128)}), s32[128,1,8]{2,1,0:T(1,128)S(1)}, u32[]{:S(2)}, u32[]{:S(2)}) %all-to-all-start) | async-done | bytes 4128 | tf_op jit(solution)/shard_map/all_to_all | solution.py:73
  24.0 4.5 %all-to-all-start.1 = ((bf16[128,8,768]{2,1,0:T(8,128)(2,1)}), bf16[128,8,768]{2,1,0:T(8,128)(2,1)S(1)}, u32[]{:S(2)}, u32[]{:S(2)}) async-start(bf16[128,8,768]{2,1,0:T(8,128)(2,1)} %fusion.15), calls=%async_computation.1 | async-start | bytes 3145728 | tf_op jit(solution)/shard_map/all_to_all | solution.py:66
  28.6 0.1 reshape.193
  28.7 0.1 convert_reduce_fusion.1
  28.8 2.9 %collective-permute-start.2 = (s32[2]{0:T(128)S(1)}, s32[2]{0:T(128)S(1)}, u32[]{:S(2)}, u32[]{:S(2)}) collective-permute-start(s32[2]{0:T(128)S(1)} %bitcast.89), channel_id=1, source_target_pairs={{0,8},{1,9},{2,10},{3,11},{4,12},{5,13},{6,14},{7,15},{8,0},{9,1},... | collective-permute-start | bytes 32 | tf_op jit(solution)/shard_map/ppermute | solution.py:15
  31.7 2.8 %collective-permute-start = (s32[2]{0:T(128)S(1)}, s32[2]{0:T(128)S(1)}, u32[]{:S(2)}, u32[]{:S(2)}) collective-permute-start(s32[2]{0:T(128)S(1)} %bitcast.90), channel_id=1, source_target_pairs={{0,64},{16,80},{32,96},{48,112},{64,0},{80,16},{96,32},{112,48},{1... | collective-permute-start | bytes 32 | tf_op jit(solution)/shard_map/ppermute | solution.py:15
  34.5 0.2 reduce_window_sum.23
  34.7 0.5 broadcast.179
  35.2 0.8 reduce.7
  36.0 0.1 reshape.192
  36.1 0.6 fusion.118
  36.7 0.6 iota_compare_fusion.29
  37.3 0.7 iota_compare_fusion.30
  38.0 0.1 fusion.55
  38.1 10.2 %collective-permute-done.2 = s32[2]{0:T(128)S(1)} collective-permute-done((s32[2]{0:T(128)S(1)}, s32[2]{0:T(128)S(1)}, u32[]{:S(2)}, u32[]{:S(2)}) %collective-permute-start.2) | collective-permute-done | bytes 40 | tf_op jit(solution)/shard_map/ppermute | solution.py:15
  48.3 0.7 fusion.116
  48.9 0.6 iota_compare_fusion.27
  49.6 0.0 collective-permute-done
  49.6 0.6 fusion.117
  50.2 0.6 iota_compare_fusion.28
  50.9 0.6 iota_compare_fusion.25
  51.5 0.6 iota_compare_fusion.26
  52.1 0.6 all-to-all-done.1
  52.7 2.0 %multiply_reduce_fusion.2 = (f32[1024]{0:T(1024)S(1)}, bf16[1024,768]{1,0:T(8,128)(2,1)S(1)}) fusion(bf16[128,8,768]{2,1,0:T(8,128)(2,1)S(1)} %all-to-all-done.1, s32[1024]{0:T(1024)S(1)} %fusion.103), kind=kOutput, calls=%fused_computation.5 | convolution fusion | flops 1614806016 | bytes 3153920 | tf_op jit(solution)/shard_map/dot_general | solution.py:90
  54.7 2.1 %collective-permute-start.3 = (bf16[2,512,768]{2,1,0:T(8,128)(2,1)S(1)}, bf16[2,512,768]{2,1,0:T(8,128)(2,1)S(1)}, u32[]{:S(2)}, u32[]{:S(2)}) collective-permute-start(bf16[2,512,768]{2,1,0:T(8,128)(2,1)S(1)} %bitcast.85), channel_id=1, source_target_pairs={{0,8},{1,9},{2,10},{3,11},{4,12},{5,13},{6,14},{7,15},{8,0},{9,1},... | collective-permute-start | bytes 4718600 | tf_op jit(solution)/shard_map/ppermute | solution.py:15
  56.8 0.9 collective-permute-start.1
  57.7 0.7 fusion.121
  58.4 0.7 fusion.119
  59.2 0.8 fusion.122
  60.0 0.6 fusion.69
  60.6 0.8 fusion.120
  61.4 0.6 fusion.71
  62.0 0.6 fusion.65
  62.6 0.6 fusion.67
  63.2 27.6 %collective-permute-done.3 = bf16[2,512,768]{2,1,0:T(8,128)(2,1)S(1)} collective-permute-done((bf16[2,512,768]{2,1,0:T(8,128)(2,1)S(1)}, bf16[2,512,768]{2,1,0:T(8,128)(2,1)S(1)}, u32[]{:S(2)}, u32[]{:S(2)}) %collective-permute-start.3) | collective-permute-done | bytes 1572896 | tf_op jit(solution)/shard_map/ppermute | solution.py:15
  90.8 0.4 multiply_reduce_fusion
  91.2 2.4 %collective-permute-done.1 = bf16[2,512,768]{2,1,0:T(8,128)(2,1)S(1)} collective-permute-done((bf16[2,512,768]{2,1,0:T(8,128)(2,1)S(1)}, bf16[2,512,768]{2,1,0:T(8,128)(2,1)S(1)}, u32[]{:S(2)}, u32[]{:S(2)}) %collective-permute-start.1) | collective-permute-done | bytes 1572896 | tf_op jit(solution)/shard_map/ppermute | solution.py:15
  93.6 0.4 multiply_reduce_fusion.1
  94.0 0.8 select_reduce_fusion.2
  94.8 0.7 select_reduce_fusion.3
  95.5 0.8 select_reduce_fusion
  96.3 0.8 select_reduce_fusion.1
  97.1 0.7 fusion.61
  97.8 0.7 fusion.63
  98.5 0.8 divide_convert_fusion.1
  99.3 0.9 divide_convert_fusion
  100.2 2.3 %fusion.16 = bf16[128,8,768]{2,1,0:T(8,128)(2,1)S(1)} fusion(bf16[512,768]{1,0:T(8,128)(2,1)S(1)} %divide_convert_fusion, bf16[512,768]{1,0:T(8,128)(2,1)S(1)} %divide_convert_fusion.1, s32[1024]{0:T(1024)S(1)} %fusion.103), kind=kOutput, calls=%fused_computation.23 | convolution fusion | flops 1615593472 | bytes 3149824 | tf_op jit(solution)/shard_map/dot_general | solution.py:43
  102.5 32.4 %all_to_all.16 = bf16[128,8,768]{2,1,0:T(8,128)(2,1)S(1)} all-to-all(bf16[128,8,768]{2,1,0:T(8,128)(2,1)S(1)} %fusion.16), channel_id=1, replica_groups=mesh['hx'=8,'hy'=16] {'hx','hy'}, dimensions={0} | all-to-all | bytes 3145728 | tf_op jit(solution)/shard_map/all_to_all | solution.py:133
  134.9 2.1 %fusion.19 = bf16[512,768]{1,0:T(8,128)(2,1)} fusion(bf16[128,8,768]{2,1,0:T(8,128)(2,1)S(1)} %all_to_all.16, s32[512]{0:T(512)S(1)} %get-tuple-element.13), kind=kOutput, calls=%fused_computation.24 | convolution fusion | flops 806223872 | bytes 2361344 | tf_op jit(solution)/shard_map/dot_general | solution.py:43
  (16 shorter events, 0.2 us)
Async XLA Ops:
  0.0 14.5 %copy-start = (bf16[512,768]{1,0:T(8,128)(2,1)S(1)}, bf16[512,768]{1,0:T(8,128)(2,1)}, u32[]{:S(2)}) copy-start(bf16[512,768]{1,0:T(8,128)(2,1)} %param.2) | copy-start | bytes 2359300
  3.0 21.0 %all-to-all-start = ((s32[128,1,8]{2,1,0:T(1,128)}), s32[128,1,8]{2,1,0:T(1,128)S(1)}, u32[]{:S(2)}, u32[]{:S(2)}) async-start(s32[128,1,8]{2,1,0:T(1,128)} %bitcast.5), calls=%async_computation | async-start | bytes 131072 | tf_op jit(solution)/shard_map/all_to_all | solution.py:73
  24.0 28.7 %all-to-all-start.1 = ((bf16[128,8,768]{2,1,0:T(8,128)(2,1)}), bf16[128,8,768]{2,1,0:T(8,128)(2,1)S(1)}, u32[]{:S(2)}, u32[]{:S(2)}) async-start(bf16[128,8,768]{2,1,0:T(8,128)(2,1)} %fusion.15), calls=%async_computation.1 | async-start | bytes 3145728 | tf_op jit(solution)/shard_map/all_to_all | solution.py:66
  28.8 19.5 %collective-permute-start.2 = (s32[2]{0:T(128)S(1)}, s32[2]{0:T(128)S(1)}, u32[]{:S(2)}, u32[]{:S(2)}) collective-permute-start(s32[2]{0:T(128)S(1)} %bitcast.89), channel_id=1, source_target_pairs={{0,8},{1,9},{2,10},{3,11},{4,12},{5,13},{6,14},{7,15},{8,0},{9,1},... | collective-permute-start | bytes 32 | tf_op jit(solution)/shard_map/ppermute | solution.py:15
  31.7 17.9 %collective-permute-start = (s32[2]{0:T(128)S(1)}, s32[2]{0:T(128)S(1)}, u32[]{:S(2)}, u32[]{:S(2)}) collective-permute-start(s32[2]{0:T(128)S(1)} %bitcast.90), channel_id=1, source_target_pairs={{0,64},{16,80},{32,96},{48,112},{64,0},{80,16},{96,32},{112,48},{1... | collective-permute-start | bytes 32 | tf_op jit(solution)/shard_map/ppermute | solution.py:15
  54.7 36.1 %collective-permute-start.3 = (bf16[2,512,768]{2,1,0:T(8,128)(2,1)S(1)}, bf16[2,512,768]{2,1,0:T(8,128)(2,1)S(1)}, u32[]{:S(2)}, u32[]{:S(2)}) collective-permute-start(bf16[2,512,768]{2,1,0:T(8,128)(2,1)S(1)} %bitcast.85), channel_id=1, source_target_pairs={{0,8},{1,9},{2,10},{3,11},{4,12},{5,13},{6,14},{7,15},{8,0},{9,1},... | collective-permute-start | bytes 4718600 | tf_op jit(solution)/shard_map/ppermute | solution.py:15
  56.8 36.8 %collective-permute-start.1 = (bf16[2,512,768]{2,1,0:T(8,128)(2,1)S(1)}, bf16[2,512,768]{2,1,0:T(8,128)(2,1)S(1)}, u32[]{:S(2)}, u32[]{:S(2)}) collective-permute-start(bf16[2,512,768]{2,1,0:T(8,128)(2,1)S(1)} %bitcast.86), channel_id=1, source_target_pairs={{0,64},{16,80},{32,96},{48,112},{64,0},{80,16},{96,32},{112,48},{1... | collective-permute-start | bytes 4718600 | tf_op jit(solution)/shard_map/ppermute | solution.py:15
where the time goes:
time: 137 us
  waiting for transfers between devices  48 us (35%)
  blocking collectives  32.4 us (24%)
  starting transfers between devices  24.7 us (18%)
  matrix products  21 us (15%)
  other arithmetic  7.36 us (5%)
  local copies, waits for them, and re-layouts  3.31 us (2%)
    ppermute x4, waiting for transfers between devices, swapped(): lax.ppermute(value, axis, [(i, i ^ 1 << apart) for i in range(lax.axis_si...  40.2 us
    all_to_all x1, blocking collectives, body(): lax.all_to_all(back_rows.reshape(device_count, slot_size, feature_width),...  32.4 us
    all_to_all x1, starting transfers between devices, body(): lax.all_to_all(send_ids.reshape(device_count, slot_size), ('hx', 'hy'), s...  11.5 us
    ppermute x4, starting transfers between devices, swapped(): lax.ppermute(value, axis, [(i, i ^ 1 << apart) for i in range(lax.axis_si...  8.66 us
    all_to_all x1, waiting for transfers between devices, body(): lax.all_to_all(send_ids.reshape(device_count, slot_size), ('hx', 'hy'), s...  7.28 us
    dot_general x8, matrix products, body(): lax.dot_general(query_rows, key_rows, (((1,), (1,)), ((), ())), preferred...  6.1 us
    dot_general x8, matrix products, body(): jnp.dot(kernel.astype(jnp.bfloat16), key_rows, preferred_element_type=jnp...  5.53 us
    all_to_all x1, starting transfers between devices, body(): lax.all_to_all(send_flat.reshape(device_count, slot_size, feature_width),...  4.53 us
  transfers between devices with their start and end apart: 6, of which 5 were waited for; matrix products, arithmetic and copies ran while one was open for 11% of the time, Pallas kernels for 0%

commit v1 on v0

v1 whole, which is shorter than its diff:
```python
import functools
import math

import jax
import jax.numpy as jnp
from jax import lax
from jax.experimental import pallas as pl
from jax.experimental.pallas import tpu as pltpu
from jax.sharding import PartitionSpec as P

MESH = pl.DeviceIdType.MESH

BPD = 2
CAP = 512
sharpness = 32.0
epsilon = 1e-06
EMPTY = 128.0
FAR = -1e30
TQ = 256


def kernel(
    count_hx,
    count_hy,
    rows_ref,
    bucket_ref,
    out_ref,
    send_buf,
    own_buf,
    hx_buf,
    hy_buf,
    back_buf,
    home_buf,
    keys,
    key_scale,
    key_bias,
    query_scale,
    numer,
    denom,
    send_sem,
    recv_sem,
    local_sem,
):
    devices = count_hx * count_hy
    files, width = rows_ref.shape
    slots = 8
    half_hx = count_hx // 2
    half_hy = count_hy // 2
    plane = 2 * count_hy
    planes = devices // plane
    my_hx = lax.axis_index("hx")
    my_hy = lax.axis_index("hy")
    me = my_hx * count_hy + my_hy
    other_hx = my_hx + 1 - 2 * (my_hx % 2)

    def owner_at(hx, hy):
        return ((hx % 2) * half_hx + hx // 2) * count_hy + hy

    my_owner = owner_at(my_hx, my_hy)

    def partner(step):
        core = step % 2
        dx = (step // 2) % 4
        dz = (step // 8) % 4
        dy = step // 32
        hx = ((my_hx // 2 + dy) % 4) * 2 + (my_hx + core) % 2
        hy = ((my_hy // 4 + dx) % 4) * 4 + (my_hy + dz) % 4
        return hx, hy

    barrier = pltpu.get_barrier_semaphore()

    def greet(step, carry):
        hx, hy = partner(step)
        pl.semaphore_signal(barrier, inc=1, device_id=(hx, hy), device_id_type=MESH)
        return carry

    lax.fori_loop(1, devices, greet, 0)

    bucket_row = bucket_ref[...]
    bucket_cols = jnp.broadcast_to(bucket_row.astype(jnp.float32), (128, files)).T
    rank = jnp.zeros((1, files), jnp.float32)
    lane = lax.broadcasted_iota(jnp.int32, (128, files), 1)
    sub = lax.broadcasted_iota(jnp.int32, (128, files), 0)
    bucket_f = bucket_row.astype(jnp.float32)
    for block in range(files // 128):
        col = bucket_cols[block * 128 : (block + 1) * 128, 0:1]
        same = (col == bucket_f) & (sub + block * 128 < lane)
        rank = rank + jnp.sum(jnp.where(same, 1.0, 0.0), axis=0, keepdims=True)
    target = bucket_f * 4.0 + rank
    slot_cols = jnp.broadcast_to(target, (128, files)).T

    rows = rows_ref[...]

    def pack(block, carry):
        place = lax.broadcasted_iota(jnp.int32, (256, files), 0) + block * 256
        match = (place.astype(jnp.float32) == target).astype(jnp.float32)
        used = jnp.sum(match, axis=1, keepdims=True)
        packed = jnp.dot(match.astype(jnp.bfloat16), rows, preferred_element_type=jnp.float32)
        packed = jnp.where(used > 0.5, packed, EMPTY)
        send_buf[pl.ds(block * 32, 32)] = packed.reshape(32, slots, width).astype(jnp.bfloat16)
        return carry

    lax.fori_loop(0, devices * slots // 256, pack, 0)

    pl.semaphore_wait(barrier, devices - 1)

    def send_own(step, carry):
        hx, hy = partner(step)
        pltpu.make_async_remote_copy(
            src_ref=send_buf.at[owner_at(hx, hy)],
            dst_ref=own_buf.at[me],
            send_sem=send_sem.at[0],
            recv_sem=recv_sem.at[0],
            device_id=(hx, hy),
            device_id_type=MESH,
        ).start()
        return carry

    def send_hy(step, carry):
        hx, hy = partner(step)
        pltpu.make_async_remote_copy(
            src_ref=send_buf.at[owner_at(hx, (hy + half_hy) % count_hy)],
            dst_ref=hy_buf.at[me],
            send_sem=send_sem.at[1],
            recv_sem=recv_sem.at[1],
            device_id=(hx, hy),
            device_id_type=MESH,
        ).start()
        return carry

    self_own = pltpu.make_async_copy(send_buf.at[my_owner], own_buf.at[me], local_sem.at[0])
    self_hy = pltpu.make_async_copy(
        send_buf.at[owner_at(my_hx, (my_hy + half_hy) % count_hy)], hy_buf.at[me], local_sem.at[1]
    )
    self_own.start()
    self_hy.start()
    lax.fori_loop(1, devices, send_own, 0)
    lax.fori_loop(1, devices, send_hy, 0)

    numer[...] = jnp.zeros_like(numer)
    denom[...] = jnp.zeros_like(denom)

    def wait_all(buf, sem):
        part = buf.at[pl.ds(0, devices - 1)]
        pltpu.make_async_copy(part, part, sem).wait()

    low = lax.broadcasted_iota(jnp.int32, (16, slots, width), 1) < 4
    fold = sharpness / width * math.log2(math.e)

    def mixed(one, two):
        first = jnp.where(low, one, pltpu.roll(two, 4, 1))
        second = jnp.where(low, pltpu.roll(one, 4, 1), two)
        return first, second

    def settle(source, base, with_query):
        def block_step(block, carry):
            taken = source[pl.ds(block * 32, 32)].astype(jnp.float32).reshape(16, 2, slots, width)
            pair = mixed(taken[:, 0], taken[:, 1])
            start = pl.multiple_of(block * 128, 128)
            for which in range(BPD):
                values = pair[which].reshape(128, width)
                square = jnp.sum(values * values, axis=1, keepdims=True)
                inverse = 1.0 / jnp.sqrt(square * (1.0 / width) + epsilon)
                used = values[:, 0:1] < 100.0
                wide = jnp.broadcast_to(jnp.where(used, inverse, -1.0), (128, 128))
                across = wide.T[0:1, :]
                keys[base + which, pl.ds(start, 128), :] = values.astype(jnp.bfloat16)
                key_scale[base + which, :, pl.ds(start, 128)] = across
                key_bias[base + which, :, pl.ds(start, 128)] = jnp.where(across > 0.0, 0.0, FAR)
                if with_query:
                    query_scale[base + which, pl.ds(start, 128), :] = jnp.broadcast_to(
                        inverse * fold, (128, 128)
                    )
            return carry

        lax.fori_loop(0, devices // 32, block_step, 0)

    def pair_tile(query, start, tile, key, skip_self):
        queries = keys[query, pl.ds(start, tile), :]
        against = keys[key]
        products = lax.dot_general(
            queries, against, (((1,), (1,)), ((), ())), preferred_element_type=jnp.float32
        )
        scale = query_scale[query, pl.ds(start, tile), :][:, 0:1]
        weight = jnp.exp2(products * scale * key_scale[key] + key_bias[key])
        if skip_self is not None:
            row = lax.broadcasted_iota(jnp.int32, (tile, CAP), 0) + start + skip_self
            col = lax.broadcasted_iota(jnp.int32, (tile, CAP), 1)
            weight = jnp.where(row == col, 0.0, weight)
        total = weight[:, 0:128]
        for part in range(1, CAP // 128):
            total = total + weight[:, part * 128 : (part + 1) * 128]
        summed = jnp.dot(weight.astype(jnp.bfloat16), against, preferred_element_type=jnp.float32)
        return summed, total

    def accumulate(query, start, tile, key, skip_self):
        summed, total = pair_tile(query, start, tile, key, skip_self)
        numer[query, pl.ds(start, tile), :] += summed
        denom[query, pl.ds(start, tile), :] += total

    wait_all(own_buf, recv_sem.at[0])
    self_own.wait()
    swap = pltpu.make_async_remote_copy(
        src_ref=own_buf,
        dst_ref=hx_buf,
        send_sem=send_sem.at[2],
        recv_sem=recv_sem.at[2],
        device_id=(other_hx, my_hy),
        device_id_type=MESH,
    )
    swap.start()
    settle(own_buf, 0, True)
    tiles = CAP // TQ

    def own_step(step, carry):
        query = step // (2 * tiles)
        key = (step // tiles) % 2
        start = pl.multiple_of((step % tiles) * TQ, TQ)
        apart = (query + key) % 2
        accumulate(query, start, TQ, key, apart * (2 * CAP))
        return carry

    lax.fori_loop(0, 4 * tiles, own_step, 0)

    swap.wait_recv()
    settle(hx_buf, 2, False)

    def hx_step(step, carry):
        query = step // tiles
        start = pl.multiple_of((step % tiles) * TQ, TQ)
        accumulate(query, start, TQ, 2 + query, None)
        return carry

    lax.fori_loop(0, 2 * tiles, hx_step, 0)

    wait_all(hy_buf, recv_sem.at[1])
    self_hy.wait()
    settle(hy_buf, 4, False)

    def last_step(step, carry):
        block = (my_hx // 2 + step) % planes
        start = pl.multiple_of(block * 128, 128)
        pieces = []
        for query in range(BPD):
            summed, total = pair_tile(query, start, 128, 4 + query, None)
            whole = numer[query, pl.ds(start, 128), :] + summed
            under = denom[query, pl.ds(start, 128), :] + total
            under = 1.0 + jnp.sum(under, axis=1, keepdims=True)
            pieces.append((whole * (1.0 / under)).reshape(16, slots, width))
        first, second = mixed(pieces[0], pieces[1])
        both = jnp.stack([first, second], axis=1).reshape(32, slots, width)
        back_buf[pl.ds(block * plane, plane)] = both.astype(jnp.bfloat16)

        def give(index, inner):
            core = index % 2
            hx = block * 2 + (my_hx + core) % 2
            dx = (index // 2) % 4
            dz = index // 8
            hy = ((my_hy // 4 + dx) % 4) * 4 + (my_hy + dz) % 4
            to = hx * count_hy + hy

            @pl.when(to != me)
            def _():
                pltpu.make_async_remote_copy(
                    src_ref=back_buf.at[to],
                    dst_ref=home_buf.at[my_owner],
                    send_sem=send_sem.at[3],
                    recv_sem=recv_sem.at[3],
                    device_id=(hx, hy),
                    device_id_type=MESH,
                ).start()

            return inner

        lax.fori_loop(0, plane, give, 0)
        return carry

    lax.fori_loop(0, planes, last_step, 0)
    self_back = pltpu.make_async_copy(back_buf.at[me], home_buf.at[my_owner], local_sem.at[2])
    self_back.start()
    self_back.wait()
    wait_all(home_buf, recv_sem.at[3])

    result = jnp.zeros((files, width), jnp.float32)
    slot_wide = jnp.concatenate([slot_cols, slot_cols], axis=1)
    place = lax.broadcasted_iota(jnp.int32, (files, 256), 1).astype(jnp.float32)
    for block in range(devices * slots // 256):
        match = (slot_wide == place + float(block * 256)).astype(jnp.float32)
        got = home_buf[pl.ds(block * 32, 32)].astype(jnp.float32).reshape(256, width)
        result = result + jnp.dot(
            match.astype(jnp.bfloat16), got.astype(jnp.bfloat16), preferred_element_type=jnp.float32
        )
    out_ref[...] = result.astype(jnp.bfloat16)

    swap.wait_send()
    wait_all(send_buf, send_sem.at[0])
    wait_all(send_buf, send_sem.at[1])
    wait_all(back_buf, send_sem.at[3])


def solution(mesh):
    count_hx = mesh.shape["hx"]
    count_hy = mesh.shape["hy"]
    devices = count_hx * count_hy

    def body(embeddings, bucket):
        files, width = embeddings.shape
        chunk = (devices, 8, width)
        return pl.pallas_call(
            functools.partial(kernel, count_hx, count_hy),
            out_shape=jax.ShapeDtypeStruct((files, width), jnp.bfloat16),
            in_specs=[pl.BlockSpec(memory_space=pltpu.VMEM)] * 2,
            out_specs=pl.BlockSpec(memory_space=pltpu.VMEM),
            scratch_shapes=[
                pltpu.VMEM(chunk, jnp.bfloat16),
                pltpu.VMEM(chunk, jnp.bfloat16),
                pltpu.VMEM(chunk, jnp.bfloat16),
                pltpu.VMEM(chunk, jnp.bfloat16),
                pltpu.VMEM(chunk, jnp.bfloat16),
                pltpu.VMEM(chunk, jnp.bfloat16),
                pltpu.VMEM((6, CAP, width), jnp.bfloat16),
                pltpu.VMEM((6, 1, CAP), jnp.float32),
                pltpu.VMEM((6, 1, CAP), jnp.float32),
                pltpu.VMEM((2, CAP, 128), jnp.float32),
                pltpu.VMEM((2, CAP, width), jnp.float32),
                pltpu.VMEM((2, CAP, 128), jnp.float32),
                pltpu.SemaphoreType.DMA((4,)),
                pltpu.SemaphoreType.DMA((4,)),
                pltpu.SemaphoreType.DMA((3,)),
            ],
            compiler_params=pltpu.CompilerParams(
                collective_id=0, has_side_effects=True, vmem_limit_bytes=60 * 1024 * 1024
            ),
        )(embeddings, bucket.reshape(1, files))

    return jax.shard_map(
        body,
        mesh=mesh,
        in_specs=(P(("hx", "hy"), None), P(("hx", "hy"))),
        out_specs=P(("hx", "hy"), None),
        check_vma=False,
    )
```

time: 137 us -> 89 us (0.65)
  Pallas kernels: 0 us -> 86.7 us
  waiting for transfers between devices: 48 us -> 0 us
  blocking collectives: 32.4 us -> 0 us
  starting transfers between devices: 24.7 us -> 0 us
  matrix products: 21 us -> 0 us
  other arithmetic: 7.36 us -> 0 us
    pallas_call x0 -> x1, Pallas kernels: none -> 86.7 us  [body(): pl.pallas_call(functools.partial(kernel, count_hx, count_hy), out_shape=j...]
    ppermute x4 -> x0, waiting for transfers between devices: 40.2 us -> none  [swapped(): lax.ppermute(value, axis, [(i, i ^ 1 << apart) for i in range(lax.axis_si...]
    all_to_all x1 -> x0, blocking collectives: 32.4 us -> none  [body(): lax.all_to_all(back_rows.reshape(device_count, slot_size, feature_width),...]
    dot_general x23 -> x0, matrix products: 21 us -> none  [the longest x8 6.1 us: body(): lax.dot_general(query_rows, key_rows, (((1,), (1,)), ((), ())), preferred...]
    all_to_all x2 -> x0, starting transfers between devices: 16 us -> none  [the longest x1 11.5 us: body(): lax.all_to_all(send_ids.reshape(device_count, slot_size), ('hx', 'hy'), s...]
    ppermute x4 -> x0, starting transfers between devices: 8.66 us -> none  [swapped(): lax.ppermute(value, axis, [(i, i ^ 1 << apart) for i in range(lax.axis_si...]
    all_to_all x2 -> x0, waiting for transfers between devices: 7.85 us -> none  [the longest x1 7.28 us: body(): lax.all_to_all(send_ids.reshape(device_count, slot_size), ('hx', 'hy'), s...]
    lt x6 -> x0, other arithmetic: 3.81 us -> none  [body(): live = jnp.broadcast_to((column_index < key_count)[None, :], score.shape)]
  transfers between devices with their start and end apart: 6 -> 0, of which waited for: 5 -> 0; matrix products, arithmetic and copies ran while one was open for 11% -> 0% of each run, Pallas kernels for 0% -> 0%
where the time goes in v1:
time: 89 us; the launch traced here: 88.8 us
  Pallas kernels  86.7 us (97%)
  local copies, waits for them, and re-layouts  2.06 us (2%)
    pallas_call x1, Pallas kernels, body(): pl.pallas_call(functools.partial(kernel, count_hx, count_hy), out_shape=j...  86.7 us
    unnamed x1, local copies, waits for them, and re-layouts  2.06 us

profile of v1, /device:TPU:1, one launch (start us, length us, event | category | flops | bytes accessed | tf_op | source)
XLA Modules:
  0.0 88.8 jit_solution(11913091881202375593)
XLA Ops:
  0.0 86.7 %shard_map.28 = bf16[512,768]{1,0:T(8,128)(2,1)} custom-call(bf16[512,768]{1,0:T(8,128)(2,1)} %rows_ref.1, s32[1,512]{1,0:T(1,128)} %bitcast.1), custom_call_target="tpu_custom_call" | custom-call | tf_op jit(solution)/shard_map/pallas_call | solution.py:309
  86.7 2.1 %copy.4 = bf16[512,768]{1,0:T(8,128)(2,1)} copy(bf16[512,768]{1,0:T(8,128)(2,1)} %shard_map.28) | data formatting | bytes 1572864

commit v2 on v1

--- a/solution.py
+++ b/solution.py
@@ -59,22 +59,24 @@
     my_owner = owner_at(my_hx, my_hy)
 
     def partner(step):
-        core = step % 2
-        dx = (step // 2) % 4
-        dz = (step // 8) % 4
-        dy = step // 32
+        core = step // 64
+        dx = step % 4
+        dy = (step // 4 + step) % 4
+        dz = (step // 16 + step // 4 + step) % 4
         hx = ((my_hx // 2 + dy) % 4) * 2 + (my_hx + core) % 2
         hy = ((my_hy // 4 + dx) % 4) * 4 + (my_hy + dz) % 4
         return hx, hy
 
     barrier = pltpu.get_barrier_semaphore()
 
-    def greet(step, carry):
-        hx, hy = partner(step)
-        pl.semaphore_signal(barrier, inc=1, device_id=(hx, hy), device_id_type=MESH)
-        return carry
-
-    lax.fori_loop(1, devices, greet, 0)
+    hxs = [(my_hx // 2 + dy) % 4 * 2 + (my_hx + core) % 2 for dy in range(4) for core in range(2)]
+    hys = [(my_hy // 4 + dx) % 4 * 4 + (my_hy + dz) % 4 for dx in range(4) for dz in range(4)]
+    for row in reversed(range(8)):
+        for column in reversed(range(16)):
+            if row or column:
+                pl.semaphore_signal(
+                    barrier, inc=1, device_id=(hxs[row], hys[column]), device_id_type=MESH
+                )
 
     bucket_row = bucket_ref[...]
     bucket_cols = jnp.broadcast_to(bucket_row.astype(jnp.float32), (128, files)).T
@@ -238,7 +240,7 @@
     settle(hy_buf, 4, False)
 
     def last_step(step, carry):
-        block = (my_hx // 2 + step) % planes
+        block = (my_hx // 2 + 2 + 3 * step) % planes
         start = pl.multiple_of(block * 128, 128)
         pieces = []
         for query in range(BPD):
@@ -252,10 +254,10 @@
         back_buf[pl.ds(block * plane, plane)] = both.astype(jnp.bfloat16)
 
         def give(index, inner):
-            core = index % 2
+            core = index // 16
             hx = block * 2 + (my_hx + core) % 2
-            dx = (index // 2) % 4
-            dz = index // 8
+            dx = (index + 2) % 4
+            dz = (index // 4 + index) % 4
             hy = ((my_hy // 4 + dx) % 4) * 4 + (my_hy + dz) % 4
             to = hx * count_hy + hy
 

time: 89 us -> 79 us (0.89)
  Pallas kernels: 86.7 us -> 76.8 us
    pallas_call x1, Pallas kernels: 86.7 us -> 76.8 us  [body(): pl.pallas_call(functools.partial(kernel, count_hx, count_hy), out_shape=j...]
where the time goes in v2:
time: 79 us; the launch traced here: 78.8 us
  Pallas kernels  76.8 us (97%)
  local copies, waits for them, and re-layouts  2.06 us (3%)
    pallas_call x1, Pallas kernels, body(): pl.pallas_call(functools.partial(kernel, count_hx, count_hy), out_shape=j...  76.8 us
    unnamed x1, local copies, waits for them, and re-layouts  2.06 us

profile of v2, /device:TPU:1, one launch (start us, length us, event | category | flops | bytes accessed | tf_op | source)
XLA Modules:
  0.0 78.8 jit_solution(15464113660427992488)
XLA Ops:
  0.0 76.8 %shard_map.28 = bf16[512,768]{1,0:T(8,128)(2,1)} custom-call(bf16[512,768]{1,0:T(8,128)(2,1)} %rows_ref.1, s32[1,512]{1,0:T(1,128)} %bitcast.1), custom_call_target="tpu_custom_call" | custom-call | tf_op jit(solution)/shard_map/pallas_call | solution.py:311
  76.8 2.1 %copy.4 = bf16[512,768]{1,0:T(8,128)(2,1)} copy(bf16[512,768]{1,0:T(8,128)(2,1)} %shard_map.28) | data formatting | bytes 1572864

commit v3 on v2

v3 whole, which is shorter than its diff:
```python
import functools
import math

import jax
import jax.numpy as jnp
from jax import lax
from jax.experimental import pallas as pl
from jax.experimental.pallas import tpu as pltpu
from jax.sharding import PartitionSpec as P

MESH = pl.DeviceIdType.MESH

CAP = 512
BUCKETS = 256
SLOTS = 4
sharpness = 32.0
epsilon = 1e-06
EMPTY = 128.0
FAR = -1e30
TQ = 256

OFFSET = {name: 128 * (name // 100) + 16 * (name // 10 % 10) + name % 10 for name in (0, 1, 10, 11, 100, 101, 110)}
DIRECT = ((0, 1, 101), (10, 100, 11, 110))


def rem(value, by):
    return lax.rem(value, jnp.int32(by))


def div(value, by):
    return lax.div(value, jnp.int32(by))


def kernel(
    rows_ref,
    bucket_ref,
    out_ref,
    send_buf,
    raw,
    back_buf,
    home_buf,
    keys,
    key_scale,
    key_bias,
    query_scale,
    numer,
    denom,
    send_sem,
    recv_sem,
    local_sem,
):
    files, width = rows_ref.shape
    devices = raw.shape[1]
    half = width // 2
    my_hx = lax.axis_index("hx")
    my_hy = lax.axis_index("hy")
    my_core = rem(my_hx, 2)
    my_y = div(my_hx, 2)
    my_x = div(my_hy, 4)
    my_z = rem(my_hy, 4)
    me = my_hx * 16 + my_hy

    def bucket_at(y, hy, name):
        offset = OFFSET[name]
        return 32 * y + 2 * rem(hy, 8) + offset + div(hy, 8) * (145 - 2 * offset)

    def chip(step):
        first, second, third = rem(step, 4), div(step, 4), div(step, 16)
        x = rem(my_x + first, 4)
        y = rem(my_y + second + first, 4)
        z = rem(my_z + third + second + first, 4)
        return y, x * 4 + z

    barrier = pltpu.get_barrier_semaphore()
    hxs = [rem(my_y + dy, 4) * 2 + rem(my_core + core, 2) for dy in range(4) for core in range(2)]
    hys = [rem(my_x + dx, 4) * 4 + rem(my_z + dz, 4) for dx in range(4) for dz in range(4)]
    for row in reversed(range(8)):
        for column in reversed(range(16)):
            if row or column:
                pl.semaphore_signal(
                    barrier, inc=1, device_id=(hxs[row], hys[column]), device_id_type=MESH
                )

    bucket_f = bucket_ref[...].astype(jnp.float32)
    bucket_cols = jnp.broadcast_to(bucket_f, (128, files)).T
    rank = jnp.zeros((1, files), jnp.float32)
    lane = lax.broadcasted_iota(jnp.int32, (128, files), 1)
    sub = lax.broadcasted_iota(jnp.int32, (128, files), 0)
    for block in range(files // 128):
        col = bucket_cols[block * 128 : (block + 1) * 128, 0:1]
        same = (col == bucket_f) & (sub + block * 128 < lane)
        rank = rank + jnp.sum(jnp.where(same, 1.0, 0.0), axis=0, keepdims=True)
    target = bucket_f * float(SLOTS) + rank
    slot_cols = jnp.broadcast_to(target, (128, files)).T

    def mixed(one, two):
        low = lax.broadcasted_iota(jnp.int32, one.shape, 1) < SLOTS
        first = jnp.where(low, one, pltpu.roll(two, SLOTS, 1))
        second = jnp.where(low, pltpu.roll(one, SLOTS, 1), two)
        return first, second

    def fold_rows(values):
        count = values.shape[0] // 8
        one, two = mixed(
            values[:, :half].reshape(count, 8, half), values[:, half:].reshape(count, 8, half)
        )
        return jnp.stack([one, two], axis=1).reshape(count * 2, 8, half).astype(jnp.bfloat16)

    def unfold_rows(packed):
        count = packed.shape[0] // 2
        halves = packed.astype(jnp.float32).reshape(count, 2, 8, half)
        first, second = mixed(halves[:, 0], halves[:, 1])
        return first.reshape(count * 8, half), second.reshape(count * 8, half)

    rows = rows_ref[...]

    def pack(block, carry):
        place = lax.broadcasted_iota(jnp.int32, (256, files), 0) + block * 256
        match = (place.astype(jnp.float32) == target).astype(jnp.float32)
        used = jnp.sum(match, axis=1, keepdims=True)
        packed = jnp.dot(match.astype(jnp.bfloat16), rows, preferred_element_type=jnp.float32)
        send_buf[pl.ds(block * 64, 64)] = fold_rows(jnp.where(used > 0.5, packed, EMPTY))
        return carry

    lax.fori_loop(0, BUCKETS * SLOTS // 256, pack, 0)

    pl.semaphore_wait(barrier, devices - 1)

    def send(y, hy, core, slot):
        pltpu.make_async_remote_copy(
            src_ref=send_buf.at[bucket_at(y, hy, DIRECT[core][slot])],
            dst_ref=raw.at[slot, me],
            send_sem=send_sem.at[slot],
            recv_sem=recv_sem.at[slot],
            device_id=(y * 2 + core, hy),
            device_id_type=MESH,
        ).start()

    def keep(core, slot):
        return pltpu.make_async_copy(
            send_buf.at[bucket_at(my_y, my_hy, DIRECT[core][slot])],
            raw.at[slot, me],
            local_sem.at[slot],
        )

    for core in range(2):

        @pl.when(my_core == core)
        def _():
            for slot in range(len(DIRECT[core])):
                keep(core, slot).start()
            for slot in range(len(DIRECT[1 - core])):
                send(my_y, my_hy, 1 - core, slot)

    def send_first(step, carry):
        y, hy = chip(step)
        for core in range(2):
            for slot in range(2):
                send(y, hy, core, slot)
        return carry

    def send_second(step, carry):
        y, hy = chip(step)
        for core in range(2):
            send(y, hy, core, 2)
        return carry

    def send_third(step, carry):
        y, hy = chip(step)
        send(y, hy, 1, 3)
        return carry

    chips = devices // 2
    lax.fori_loop(1, chips, send_first, 0)
    lax.fori_loop(1, chips, send_second, 0)
    lax.fori_loop(1, chips, send_third, 0)

    def wait_count(buf, count, sem):
        part = buf.at[pl.ds(0, count)]
        pltpu.make_async_copy(part, part, sem).wait()

    def wait_slot(slot):
        wait_count(raw.at[slot], devices - 1, recv_sem.at[slot])

    def share(slot, there, sem):
        return pltpu.make_async_remote_copy(
            src_ref=raw.at[slot],
            dst_ref=raw.at[there],
            send_sem=send_sem.at[sem],
            recv_sem=recv_sem.at[there],
            device_id=(my_y * 2 + 1 - my_core, my_hy),
            device_id_type=MESH,
        )

    def wait_shared(slot):
        wait_count(raw.at[slot], devices, recv_sem.at[slot])

    scale_fold = sharpness / width * math.log2(math.e)

    def settle(slot, with_query):
        def block_step(block, carry):
            first, second = unfold_rows(raw[slot, pl.ds(block * 32, 32)])
            start = pl.multiple_of(block * 128, 128)
            square = jnp.sum(first * first + second * second, axis=1, keepdims=True)
            inverse = 1.0 / jnp.sqrt(square * (1.0 / width) + epsilon)
            used = first[:, 0:1] < 100.0
            wide = jnp.broadcast_to(jnp.where(used, inverse, -1.0), (128, 128))
            across = wide.T[0:1, :]
            keys[slot, pl.ds(start, 128), 0:half] = first.astype(jnp.bfloat16)
            keys[slot, pl.ds(start, 128), half:width] = second.astype(jnp.bfloat16)
            key_scale[slot, :, pl.ds(start, 128)] = across
            key_bias[slot, :, pl.ds(start, 128)] = jnp.where(across > 0.0, 0.0, FAR)
            if with_query:
                query_scale[slot, pl.ds(start, 128), :] = jnp.broadcast_to(
                    inverse * scale_fold, (128, 128)
                )
            return carry

        lax.fori_loop(0, devices // 32, block_step, 0)

    def pair_tile(query, start, tile, key, skip_self):
        queries = keys[query, pl.ds(start, tile), :]
        against = keys[key]
        products = lax.dot_general(
            queries, against, (((1,), (1,)), ((), ())), preferred_element_type=jnp.float32
        )
        scale = query_scale[query, pl.ds(start, tile), :][:, 0:1]
        weight = jnp.exp2(products * scale * key_scale[key] + key_bias[key])
        if skip_self:
            row = lax.broadcasted_iota(jnp.int32, (tile, CAP), 0) + start
            col = lax.broadcasted_iota(jnp.int32, (tile, CAP), 1)
            weight = jnp.where(row == col, 0.0, weight)
        total = weight[:, 0:128]
        for part in range(1, CAP // 128):
            total = total + weight[:, part * 128 : (part + 1) * 128]
        summed = jnp.dot(weight.astype(jnp.bfloat16), against, preferred_element_type=jnp.float32)
        return summed, total

    tiles = CAP // TQ

    def own_pairs():
        def step_of(step, carry):
            query = div(step, tiles)
            start = pl.multiple_of(rem(step, tiles) * TQ, TQ)
            summed, total = pair_tile(query, start, TQ, query, True)
            numer[query, pl.ds(start, TQ), :] = summed
            denom[query, pl.ds(start, TQ), :] = total
            return carry

        lax.fori_loop(0, 2 * tiles, step_of, 0)

    def pairs(count, which):
        def step_of(step, carry):
            query, key = which(div(step, tiles))
            start = pl.multiple_of(rem(step, tiles) * TQ, TQ)
            summed, total = pair_tile(query, start, TQ, key, False)
            numer[query, pl.ds(start, TQ), :] += summed
            denom[query, pl.ds(start, TQ), :] += total
            return carry

        lax.fori_loop(0, count * tiles, step_of, 0)

    def finish(query, key, name):
        mine = bucket_at(my_y, my_hy, name)

        def block_step(step, carry):
            y = rem(my_y + 2 + 3 * step, 4)
            start = pl.multiple_of(y * 128, 128)
            summed, total = pair_tile(query, start, 128, key, False)
            whole = numer[query, pl.ds(start, 128), :] + summed
            under = denom[query, pl.ds(start, 128), :] + total
            under = 1.0 + jnp.sum(under, axis=1, keepdims=True)
            back_buf[query, pl.ds(y * 32, 32)] = fold_rows(whole * (1.0 / under))

            def give(index, inner):
                x = rem(my_x + 2 + index, 4)
                z = rem(my_z + div(index, 4) + index, 4)
                hy = x * 4 + z
                for core in range(2):
                    to = (y * 2 + core) * 16 + hy

                    @pl.when(to != me)
                    def _():
                        pltpu.make_async_remote_copy(
                            src_ref=back_buf.at[query, to],
                            dst_ref=home_buf.at[mine],
                            send_sem=send_sem.at[7 + query],
                            recv_sem=recv_sem.at[6],
                            device_id=(y * 2 + core, hy),
                            device_id_type=MESH,
                        ).start()

                return inner

            lax.fori_loop(0, 16, give, 0)
            return carry

        lax.fori_loop(0, 4, block_step, 0)
        return pltpu.make_async_copy(back_buf.at[query, me], home_buf.at[mine], local_sem.at[4 + query])

    for slot in range(2):
        wait_slot(slot)
        keep(0, slot).wait()

    for core in range(2):

        @pl.when(my_core == core)
        def _():
            if core == 0:
                first_share = [share(0, 4, 4)]
            else:
                first_share = [share(0, 3, 4), share(1, 4, 5)]
            for copy in first_share:
                copy.start()
            settle(0, True)
            settle(1, True)
            own_pairs()
            if core == 0:
                pairs(2, lambda index: (index, 1 - index))
                wait_shared(3)
                settle(3, False)
                pairs(1, lambda index: (0, 3))
                wait_shared(4)
                settle(4, False)
                kept = [finish(0, 4, DIRECT[0][0])]
                kept[0].start()
                wait_slot(2)
                keep(0, 2).wait()
                second_share = share(2, 5, 6)
                second_share.start()
                settle(2, False)
                pairs(1, lambda index: (1, 2))
                wait_shared(5)
                settle(5, False)
                kept.append(finish(1, 5, DIRECT[0][1]))
                kept[1].start()
            else:
                wait_shared(4)
                settle(4, False)
                pairs(2, lambda index: (index, 4))
                wait_slot(2)
                keep(1, 2).wait()
                second_share = share(2, 5, 6)
                second_share.start()
                settle(2, False)
                pairs(1, lambda index: (0, 2))
                wait_shared(5)
                settle(5, False)
                pairs(1, lambda index: (1, 5))
                wait_slot(3)
                keep(1, 3).wait()
                settle(3, False)
                kept = [finish(0, 3, DIRECT[1][0])]
                kept[0].start()
                kept.append(finish(1, 3, DIRECT[1][1]))
                kept[1].start()
            for copy in kept:
                copy.wait()
            for copy in first_share:
                copy.wait_send()
            second_share.wait_send()

    got = home_buf.at[pl.ds(0, BUCKETS - 2)]
    pltpu.make_async_copy(got, got, recv_sem.at[6]).wait()

    slot_wide = jnp.concatenate([slot_cols, slot_cols], axis=1)
    place = lax.broadcasted_iota(jnp.int32, (files, 256), 1).astype(jnp.float32)
    results = [jnp.zeros((files, half), jnp.float32) for _ in range(2)]
    for block in range(BUCKETS * SLOTS // 256):
        match = (slot_wide == place + float(block * 256)).astype(jnp.float32).astype(jnp.bfloat16)
        parts = unfold_rows(home_buf[pl.ds(block * 64, 64)])
        results = [
            result + jnp.dot(match, part.astype(jnp.bfloat16), preferred_element_type=jnp.float32)
            for result, part in zip(results, parts)
        ]
    out_ref[:, 0:half] = results[0].astype(jnp.bfloat16)
    out_ref[:, half:width] = results[1].astype(jnp.bfloat16)

    for slot in range(3):
        wait_count(raw.at[slot], devices - 1, send_sem.at[slot])
    for core in range(2):

        @pl.when(my_core == core)
        def _():
            wait_count(raw.at[3], chips - core, send_sem.at[3])

    for query in range(2):
        wait_count(raw.at[query], devices - 1, send_sem.at[7 + query])


def solution(mesh):
    devices = mesh.shape["hx"] * mesh.shape["hy"]

    def body(embeddings, bucket):
        files, width = embeddings.shape
        half = width // 2
        return pl.pallas_call(
            kernel,
            out_shape=jax.ShapeDtypeStruct((files, width), jnp.bfloat16),
            in_specs=[pl.BlockSpec(memory_space=pltpu.VMEM)] * 2,
            out_specs=pl.BlockSpec(memory_space=pltpu.VMEM),
            scratch_shapes=[
                pltpu.VMEM((BUCKETS, 8, half), jnp.bfloat16),
                pltpu.VMEM((6, devices, 8, half), jnp.bfloat16),
                pltpu.VMEM((2, devices, 8, half), jnp.bfloat16),
                pltpu.VMEM((BUCKETS, 8, half), jnp.bfloat16),
                pltpu.VMEM((6, CAP, width), jnp.bfloat16),
                pltpu.VMEM((6, 1, CAP), jnp.float32),
                pltpu.VMEM((6, 1, CAP), jnp.float32),
                pltpu.VMEM((2, CAP, 128), jnp.float32),
                pltpu.VMEM((2, CAP, width), jnp.float32),
                pltpu.VMEM((2, CAP, 128), jnp.float32),
                pltpu.SemaphoreType.DMA((9,)),
                pltpu.SemaphoreType.DMA((7,)),
                pltpu.SemaphoreType.DMA((6,)),
            ],
            compiler_params=pltpu.CompilerParams(
                collective_id=0, has_side_effects=True, vmem_limit_bytes=60 * 1024 * 1024
            ),
        )(embeddings, bucket.reshape(1, files))

    return jax.shard_map(
        body,
        mesh=mesh,
        in_specs=(P(("hx", "hy"), None), P(("hx", "hy"))),
        out_specs=P(("hx", "hy"), None),
        check_vma=False,
    )
```

time: 79 us -> 80.6 us (1.020)
  Pallas kernels: 76.8 us -> 77.7 us
    pallas_call x1, Pallas kernels: 76.8 us -> 77.7 us  [body(): pl.pallas_call(kernel, out_shape=jax.ShapeDtypeStruct((files, width), jnp...]
where the time goes in v3:
time: 80.6 us; the launch traced here: 79.7 us
  Pallas kernels  77.7 us (96%)
  local copies, waits for them, and re-layouts  2.06 us (3%)
    pallas_call x1, Pallas kernels, body(): pl.pallas_call(kernel, out_shape=jax.ShapeDtypeStruct((files, width), jnp...  77.7 us
    unnamed x1, local copies, waits for them, and re-layouts  2.06 us

profile of v3, /device:TPU:1, one launch (start us, length us, event | category | flops | bytes accessed | tf_op | source)
XLA Modules:
  0.0 79.7 jit_solution(8544934019608639447)
XLA Ops:
  0.0 77.7 %shard_map.28 = bf16[512,768]{1,0:T(8,128)(2,1)} custom-call(bf16[512,768]{1,0:T(8,128)(2,1)} %rows_ref.1, s32[1,512]{1,0:T(1,128)} %bitcast.1), custom_call_target="tpu_custom_call" | custom-call | tf_op jit(solution)/shard_map/pallas_call | solution.py:397
  77.7 2.1 %copy.4 = bf16[512,768]{1,0:T(8,128)(2,1)} copy(bf16[512,768]{1,0:T(8,128)(2,1)} %shard_map.28) | data formatting | bytes 1572864

commit v4 on v3

--- a/solution.py
+++ b/solution.py
@@ -17,7 +17,7 @@
 epsilon = 1e-06
 EMPTY = 128.0
 FAR = -1e30
-TQ = 256
+SPAN = 64
 
 OFFSET = {name: 128 * (name // 100) + 16 * (name // 10 % 10) + name % 10 for name in (0, 1, 10, 11, 100, 101, 110)}
 DIRECT = ((0, 1, 101), (10, 100, 11, 110))
@@ -64,13 +64,6 @@
         offset = OFFSET[name]
         return 32 * y + 2 * rem(hy, 8) + offset + div(hy, 8) * (145 - 2 * offset)
 
-    def chip(step):
-        first, second, third = rem(step, 4), div(step, 4), div(step, 16)
-        x = rem(my_x + first, 4)
-        y = rem(my_y + second + first, 4)
-        z = rem(my_z + third + second + first, 4)
-        return y, x * 4 + z
-
     barrier = pltpu.get_barrier_semaphore()
     hxs = [rem(my_y + dy, 4) * 2 + rem(my_core + core, 2) for dy in range(4) for core in range(2)]
     hys = [rem(my_x + dx, 4) * 4 + rem(my_z + dz, 4) for dx in range(4) for dz in range(4)]
@@ -126,13 +119,20 @@
 
     pl.semaphore_wait(barrier, devices - 1)
 
-    def send(y, hy, core, slot):
+    hy_low = [2 * rem(hy, 8) for hy in hys]
+    hy_flip = [div(hy, 8) for hy in hys]
+    cross = [(column // 4 + column) % 4 for column in range(16)]
+
+    def send(y, column, core, slot):
+        offset = OFFSET[DIRECT[core][slot]]
         pltpu.make_async_remote_copy(
-            src_ref=send_buf.at[bucket_at(y, hy, DIRECT[core][slot])],
+            src_ref=send_buf.at[
+                32 * y + hy_low[column] + offset + hy_flip[column] * (145 - 2 * offset)
+            ],
             dst_ref=raw.at[slot, me],
             send_sem=send_sem.at[slot],
             recv_sem=recv_sem.at[slot],
-            device_id=(y * 2 + core, hy),
+            device_id=(y * 2 + core, hys[column]),
             device_id_type=MESH,
         ).start()
 
@@ -150,30 +150,29 @@
             for slot in range(len(DIRECT[core])):
                 keep(core, slot).start()
             for slot in range(len(DIRECT[1 - core])):
-                send(my_y, my_hy, 1 - core, slot)
-
-    def send_first(step, carry):
-        y, hy = chip(step)
-        for core in range(2):
-            for slot in range(2):
-                send(y, hy, core, slot)
-        return carry
-
-    def send_second(step, carry):
-        y, hy = chip(step)
-        for core in range(2):
-            send(y, hy, core, 2)
-        return carry
-
-    def send_third(step, carry):
-        y, hy = chip(step)
-        send(y, hy, 1, 3)
-        return carry
+                send(my_y, 0, 1 - core, slot)
+
+    def send_slot(slot, cores):
+        def around(turn, carry):
+            ys = [rem(my_y + turn + shift, 4) for shift in range(4)]
+            for column in reversed(range(1, 16)):
+                for core in cores:
+                    send(ys[cross[column]], column, core, slot)
+
+            @pl.when(turn > 0)
+            def _():
+                for core in cores:
+                    send(ys[0], 0, core, slot)
+
+            return carry
+
+        lax.fori_loop(0, 4, around, 0)
 
     chips = devices // 2
-    lax.fori_loop(1, chips, send_first, 0)
-    lax.fori_loop(1, chips, send_second, 0)
-    lax.fori_loop(1, chips, send_third, 0)
+    send_slot(0, (0, 1))
+    send_slot(1, (0, 1))
+    send_slot(2, (0, 1))
+    send_slot(3, (1,))
 
     def wait_count(buf, count, sem):
         part = buf.at[pl.ds(0, count)]
@@ -199,24 +198,24 @@
 
     def settle(slot, with_query):
         def block_step(block, carry):
-            first, second = unfold_rows(raw[slot, pl.ds(block * 32, 32)])
-            start = pl.multiple_of(block * 128, 128)
+            first, second = unfold_rows(raw[slot, pl.ds(block * SPAN, SPAN)])
+            start = pl.multiple_of(block * (SPAN * 4), SPAN * 4)
             square = jnp.sum(first * first + second * second, axis=1, keepdims=True)
             inverse = 1.0 / jnp.sqrt(square * (1.0 / width) + epsilon)
             used = first[:, 0:1] < 100.0
-            wide = jnp.broadcast_to(jnp.where(used, inverse, -1.0), (128, 128))
+            wide = jnp.broadcast_to(jnp.where(used, inverse, -1.0), (SPAN * 4, 128))
             across = wide.T[0:1, :]
-            keys[slot, pl.ds(start, 128), 0:half] = first.astype(jnp.bfloat16)
-            keys[slot, pl.ds(start, 128), half:width] = second.astype(jnp.bfloat16)
-            key_scale[slot, :, pl.ds(start, 128)] = across
-            key_bias[slot, :, pl.ds(start, 128)] = jnp.where(across > 0.0, 0.0, FAR)
+            keys[slot, pl.ds(start, SPAN * 4), 0:half] = first.astype(jnp.bfloat16)
+            keys[slot, pl.ds(start, SPAN * 4), half:width] = second.astype(jnp.bfloat16)
+            key_scale[slot, :, pl.ds(start, SPAN * 4)] = across
+            key_bias[slot, :, pl.ds(start, SPAN * 4)] = jnp.where(across > 0.0, 0.0, FAR)
             if with_query:
-                query_scale[slot, pl.ds(start, 128), :] = jnp.broadcast_to(
-                    inverse * scale_fold, (128, 128)
+                query_scale[slot, pl.ds(start, SPAN * 4), :] = jnp.broadcast_to(
+                    inverse * scale_fold, (SPAN * 4, 128)
                 )
             return carry
 
-        lax.fori_loop(0, devices // 32, block_step, 0)
+        lax.fori_loop(0, devices // SPAN, block_step, 0)
 
     def pair_tile(query, start, tile, key, skip_self):
         queries = keys[query, pl.ds(start, tile), :]
@@ -236,129 +235,122 @@
         summed = jnp.dot(weight.astype(jnp.bfloat16), against, preferred_element_type=jnp.float32)
         return summed, total
 
-    tiles = CAP // TQ
-
-    def own_pairs():
-        def step_of(step, carry):
-            query = div(step, tiles)
-            start = pl.multiple_of(rem(step, tiles) * TQ, TQ)
-            summed, total = pair_tile(query, start, TQ, query, True)
-            numer[query, pl.ds(start, TQ), :] = summed
-            denom[query, pl.ds(start, TQ), :] = total
+    def own_pair(query):
+        summed, total = pair_tile(query, 0, CAP, query, True)
+        numer[query] = summed
+        denom[query] = total
+
+    def pair(query, key):
+        summed, total = pair_tile(query, 0, CAP, key, False)
+        numer[query] += summed
+        denom[query] += total
+
+    def my_bucket(query):
+        offset = query + my_core * (16 + 111 * query)
+        return 32 * my_y + 2 * rem(my_hy, 8) + offset + div(my_hy, 8) * (145 - 2 * offset)
+
+    def keep_back(query):
+        return pltpu.make_async_copy(
+            back_buf.at[query, me], home_buf.at[my_bucket(query)], local_sem.at[4 + query]
+        )
+
+    def finish(query, key):
+        mine = my_bucket(query)
+
+        def block_step(step, carry):
+            upper = rem(div(my_y, 2) + 1 + step, 2)
+            start = pl.multiple_of(upper * 256, 256)
+            summed, total = pair_tile(query, start, 256, key, False)
+            whole = numer[query, pl.ds(start, 256), :] + summed
+            under = denom[query, pl.ds(start, 256), :] + total
+            under = 1.0 + jnp.sum(under, axis=1, keepdims=True)
+            back_buf[query, pl.ds(upper * 64, 64)] = fold_rows(whole * (1.0 / under))
+
+            def give(turn, inner):
+                y = 2 * upper + rem(my_y + 1 + turn, 2)
+                for column in reversed(range(16)):
+                    for core in range(2):
+                        to = (y * 2 + core) * 16 + hys[column]
+
+                        def start_copy():
+                            pltpu.make_async_remote_copy(
+                                src_ref=back_buf.at[query, to],
+                                dst_ref=home_buf.at[mine],
+                                send_sem=send_sem.at[7 + query],
+                                recv_sem=recv_sem.at[6],
+                                device_id=(y * 2 + core, hys[column]),
+                                device_id_type=MESH,
+                            ).start()
+
+                        if column:
+                            start_copy()
+                        else:
+                            pl.when(to != me)(start_copy)
+                return inner
+
+            lax.fori_loop(0, 2, give, 0)
             return carry
 
-        lax.fori_loop(0, 2 * tiles, step_of, 0)
-
-    def pairs(count, which):
-        def step_of(step, carry):
-            query, key = which(div(step, tiles))
-            start = pl.multiple_of(rem(step, tiles) * TQ, TQ)
-            summed, total = pair_tile(query, start, TQ, key, False)
-            numer[query, pl.ds(start, TQ), :] += summed
-            denom[query, pl.ds(start, TQ), :] += total
-            return carry
-
-        lax.fori_loop(0, count * tiles, step_of, 0)
-
-    def finish(query, key, name):
-        mine = bucket_at(my_y, my_hy, name)
-
-        def block_step(step, carry):
-            y = rem(my_y + 2 + 3 * step, 4)
-            start = pl.multiple_of(y * 128, 128)
-            summed, total = pair_tile(query, start, 128, key, False)
-            whole = numer[query, pl.ds(start, 128), :] + summed
-            under = denom[query, pl.ds(start, 128), :] + total
-            under = 1.0 + jnp.sum(under, axis=1, keepdims=True)
-            back_buf[query, pl.ds(y * 32, 32)] = fold_rows(whole * (1.0 / under))
-
-            def give(index, inner):
-                x = rem(my_x + 2 + index, 4)
-                z = rem(my_z + div(index, 4) + index, 4)
-                hy = x * 4 + z
-                for core in range(2):
-                    to = (y * 2 + core) * 16 + hy
-
-                    @pl.when(to != me)
-                    def _():
-                        pltpu.make_async_remote_copy(
-                            src_ref=back_buf.at[query, to],
-                            dst_ref=home_buf.at[mine],
-                            send_sem=send_sem.at[7 + query],
-                            recv_sem=recv_sem.at[6],
-                            device_id=(y * 2 + core, hy),
-                            device_id_type=MESH,
-                        ).start()
-
-                return inner
-
-            lax.fori_loop(0, 16, give, 0)
-            return carry
-
-        lax.fori_loop(0, 4, block_step, 0)
-        return pltpu.make_async_copy(back_buf.at[query, me], home_buf.at[mine], local_sem.at[4 + query])
-
-    for slot in range(2):
-        wait_slot(slot)
-        keep(0, slot).wait()
-
-    for core in range(2):
-
-        @pl.when(my_core == core)
-        def _():
-            if core == 0:
-                first_share = [share(0, 4, 4)]
-            else:
-                first_share = [share(0, 3, 4), share(1, 4, 5)]
-            for copy in first_share:
-                copy.start()
-            settle(0, True)
-            settle(1, True)
-            own_pairs()
-            if core == 0:
-                pairs(2, lambda index: (index, 1 - index))
-                wait_shared(3)
-                settle(3, False)
-                pairs(1, lambda index: (0, 3))
-                wait_shared(4)
-                settle(4, False)
-                kept = [finish(0, 4, DIRECT[0][0])]
-                kept[0].start()
-                wait_slot(2)
-                keep(0, 2).wait()
-                second_share = share(2, 5, 6)
-                second_share.start()
-                settle(2, False)
-                pairs(1, lambda index: (1, 2))
-                wait_shared(5)
-                settle(5, False)
-                kept.append(finish(1, 5, DIRECT[0][1]))
-                kept[1].start()
-            else:
-                wait_shared(4)
-                settle(4, False)
-                pairs(2, lambda index: (index, 4))
-                wait_slot(2)
-                keep(1, 2).wait()
-                second_share = share(2, 5, 6)
-                second_share.start()
-                settle(2, False)
-                pairs(1, lambda index: (0, 2))
-                wait_shared(5)
-                settle(5, False)
-                pairs(1, lambda index: (1, 5))
-                wait_slot(3)
-                keep(1, 3).wait()
-                settle(3, False)
-                kept = [finish(0, 3, DIRECT[1][0])]
-                kept[0].start()
-                kept.append(finish(1, 3, DIRECT[1][1]))
-                kept[1].start()
-            for copy in kept:
-                copy.wait()
-            for copy in first_share:
-                copy.wait_send()
-            second_share.wait_send()
+        lax.fori_loop(0, 2, block_step, 0)
+        keep_back(query).start()
+
+    wait_slot(0)
+    keep(0, 0).wait()
+    first_share = share(0, 4 - my_core, 4)
+    first_share.start()
+    settle(0, True)
+    own_pair(0)
+    given = 3 + my_core
+    wait_shared(given)
+    settle(given, False)
+    pair(0, given)
+    wait_slot(1)
+    keep(0, 1).wait()
+
+    @pl.when(my_core == 1)
+    def _():
+        share(1, 4, 5).start()
+
+    settle(1, True)
+
+    @pl.when(my_core == 0)
+    def _():
+        pair(0, 1)
+        wait_shared(4)
+        settle(4, False)
+        finish(0, 4)
+
+    own_pair(1)
+    pair(1, 4 * my_core)
+    wait_slot(2)
+    keep(0, 2).wait()
+    second_share = share(2, 5, 6)
+    second_share.start()
+    settle(2, False)
+    pair(1 - my_core, 2)
+    wait_shared(5)
+    settle(5, False)
+
+    @pl.when(my_core == 1)
+    def _():
+        pair(1, 5)
+        wait_slot(3)
+        keep(1, 3).wait()
+        settle(3, False)
+
+    def last(index, carry):
+        finish(1 - my_core + index, 5 - 2 * my_core)
+        return carry
+
+    lax.fori_loop(0, 1 + my_core, last, 0)
+    keep_back(0).wait()
+    keep_back(1).wait()
+    first_share.wait_send()
+    second_share.wait_send()
+
+    @pl.when(my_core == 1)
+    def _():
+        share(1, 4, 5).wait_send()
 
     got = home_buf.at[pl.ds(0, BUCKETS - 2)]
     pltpu.make_async_copy(got, got, recv_sem.at[6]).wait()

time: 80.6 us -> 68.2 us (0.85)
  Pallas kernels: 77.7 us -> 65.9 us
    pallas_call x1, Pallas kernels: 77.7 us -> 65.9 us  [body(): pl.pallas_call(kernel, out_shape=jax.ShapeDtypeStruct((files, width), jnp...]
where the time goes in v4:
time: 68.2 us; the launch traced here: 68 us
  Pallas kernels  65.9 us (97%)
  local copies, waits for them, and re-layouts  2.06 us (3%)
    pallas_call x1, Pallas kernels, body(): pl.pallas_call(kernel, out_shape=jax.ShapeDtypeStruct((files, width), jnp...  65.9 us
    unnamed x1, local copies, waits for them, and re-layouts  2.06 us

profile of v4, /device:TPU:1, one launch (start us, length us, event | category | flops | bytes accessed | tf_op | source)
XLA Modules:
  0.0 68.0 jit_solution(3028910297866157580)
XLA Ops:
  0.0 65.9 %shard_map.28 = bf16[512,768]{1,0:T(8,128)(2,1)} custom-call(bf16[512,768]{1,0:T(8,128)(2,1)} %rows_ref.1, s32[1,512]{1,0:T(1,128)} %bitcast.1), custom_call_target="tpu_custom_call" | custom-call | tf_op jit(solution)/shard_map/pallas_call | solution.py:389
  65.9 2.1 %copy.4 = bf16[512,768]{1,0:T(8,128)(2,1)} copy(bf16[512,768]{1,0:T(8,128)(2,1)} %shard_map.28) | data formatting | bytes 1572864

commit v5 on v4

--- a/solution.py
+++ b/solution.py
@@ -31,10 +31,16 @@
     return lax.div(value, jnp.int32(by))
 
 
+def apart(shift):
+    return min(shift, 4 - shift)
+
+
 def kernel(
+    rows_hbm,
+    bucket_hbm,
+    out_ref,
     rows_ref,
     bucket_ref,
-    out_ref,
     send_buf,
     raw,
     back_buf,
@@ -49,7 +55,7 @@
     recv_sem,
     local_sem,
 ):
-    files, width = rows_ref.shape
+    files, width = rows_hbm.shape
     devices = raw.shape[1]
     half = width // 2
     my_hx = lax.axis_index("hx")
@@ -67,12 +73,19 @@
     barrier = pltpu.get_barrier_semaphore()
     hxs = [rem(my_y + dy, 4) * 2 + rem(my_core + core, 2) for dy in range(4) for core in range(2)]
     hys = [rem(my_x + dx, 4) * 4 + rem(my_z + dz, 4) for dx in range(4) for dz in range(4)]
-    for row in reversed(range(8)):
-        for column in reversed(range(16)):
-            if row or column:
-                pl.semaphore_signal(
-                    barrier, inc=1, device_id=(hxs[row], hys[column]), device_id_type=MESH
-                )
+    far_first = sorted(
+        ((row, column) for row in range(8) for column in range(16) if row or column),
+        key=lambda at: -(apart(at[0] // 2) + apart(at[1] // 4) + apart(at[1] % 4)),
+    )
+    for row, column in far_first:
+        pl.semaphore_signal(
+            barrier, inc=1, device_id=(hxs[row], hys[column]), device_id_type=MESH
+        )
+    fetch = pltpu.make_async_copy(rows_hbm, rows_ref, local_sem.at[6])
+    fetch.start()
+    fetch_bucket = pltpu.make_async_copy(bucket_hbm, bucket_ref, local_sem.at[7])
+    fetch_bucket.start()
+    fetch_bucket.wait()
 
     bucket_f = bucket_ref[...].astype(jnp.float32)
     bucket_cols = jnp.broadcast_to(bucket_f, (128, files)).T
@@ -105,6 +118,7 @@
         first, second = mixed(halves[:, 0], halves[:, 1])
         return first.reshape(count * 8, half), second.reshape(count * 8, half)
 
+    fetch.wait()
     rows = rows_ref[...]
 
     def pack(block, carry):
@@ -389,9 +403,11 @@
         return pl.pallas_call(
             kernel,
             out_shape=jax.ShapeDtypeStruct((files, width), jnp.bfloat16),
-            in_specs=[pl.BlockSpec(memory_space=pltpu.VMEM)] * 2,
+            in_specs=[pl.BlockSpec(memory_space=pltpu.HBM)] * 2,
             out_specs=pl.BlockSpec(memory_space=pltpu.VMEM),
             scratch_shapes=[
+                pltpu.VMEM((files, width), jnp.bfloat16),
+                pltpu.VMEM((1, files), jnp.int32),
                 pltpu.VMEM((BUCKETS, 8, half), jnp.bfloat16),
                 pltpu.VMEM((6, devices, 8, half), jnp.bfloat16),
                 pltpu.VMEM((2, devices, 8, half), jnp.bfloat16),
@@ -404,12 +420,15 @@
                 pltpu.VMEM((2, CAP, 128), jnp.float32),
                 pltpu.SemaphoreType.DMA((9,)),
                 pltpu.SemaphoreType.DMA((7,)),
-                pltpu.SemaphoreType.DMA((6,)),
+                pltpu.SemaphoreType.DMA((8,)),
             ],
             compiler_params=pltpu.CompilerParams(
-                collective_id=0, has_side_effects=True, vmem_limit_bytes=60 * 1024 * 1024
+                collective_id=0, has_side_effects=True, vmem_limit_bytes=32 * 1024 * 1024
             ),
-        )(embeddings, bucket.reshape(1, files))
+        )(
+            pltpu.with_memory_space_constraint(embeddings, pltpu.HBM),
+            pltpu.with_memory_space_constraint(bucket.reshape(1, files), pltpu.HBM),
+        )
 
     return jax.shard_map(
         body,

time: 68.2 us -> 67.3 us (0.987)
  local copies, waits for them, and re-layouts: 2.06 us -> 0.88 us
    unnamed x1, local copies, waits for them, and re-layouts: 2.06 us -> 0.88 us
where the time goes in v5:
time: 67.3 us; the launch traced here: 67.2 us
  Pallas kernels  66.3 us (99%)
  local copies, waits for them, and re-layouts  0.88 us (1%)
    pallas_call x1, Pallas kernels, body(): pl.pallas_call(kernel, out_shape=jax.ShapeDtypeStruct((files, width), jnp...  66.3 us

profile of v5, /device:TPU:1, one launch (start us, length us, event | category | flops | bytes accessed | tf_op | source)
XLA Modules:
  0.0 67.2 jit_solution(9809189650194253740)
XLA Ops:
  0.0 66.3 %shard_map.28 = bf16[512,768]{1,0:T(8,128)(2,1)S(1)} custom-call(bf16[512,768]{1,0:T(8,128)(2,1)} %rows_hbm.1, s32[1,512]{1,0:T(1,128)} %bitcast.1), custom_call_target="tpu_custom_call" | custom-call | tf_op jit(solution)/shard_map/pallas_call | solution.py:403
  66.3 0.9 %copy.4 = bf16[512,768]{1,0:T(8,128)(2,1)} copy(bf16[512,768]{1,0:T(8,128)(2,1)S(1)} %shard_map.28) | data formatting | bytes 1572864

commit v6 on v5

--- a/solution.py
+++ b/solution.py
@@ -70,6 +70,10 @@
         offset = OFFSET[name]
         return 32 * y + 2 * rem(hy, 8) + offset + div(hy, 8) * (145 - 2 * offset)
 
+    fetch_bucket = pltpu.make_async_copy(bucket_hbm, bucket_ref, local_sem.at[7])
+    fetch_bucket.start()
+    fetch = pltpu.make_async_copy(rows_hbm, rows_ref, local_sem.at[6])
+    fetch.start()
     barrier = pltpu.get_barrier_semaphore()
     hxs = [rem(my_y + dy, 4) * 2 + rem(my_core + core, 2) for dy in range(4) for core in range(2)]
     hys = [rem(my_x + dx, 4) * 4 + rem(my_z + dz, 4) for dx in range(4) for dz in range(4)]
@@ -81,10 +85,6 @@
         pl.semaphore_signal(
             barrier, inc=1, device_id=(hxs[row], hys[column]), device_id_type=MESH
         )
-    fetch = pltpu.make_async_copy(rows_hbm, rows_ref, local_sem.at[6])
-    fetch.start()
-    fetch_bucket = pltpu.make_async_copy(bucket_hbm, bucket_ref, local_sem.at[7])
-    fetch_bucket.start()
     fetch_bucket.wait()
 
     bucket_f = bucket_ref[...].astype(jnp.float32)

time: 67.3 us -> 64.5 us (0.958)
  Pallas kernels: 66.3 us -> 63.5 us
    pallas_call x1, Pallas kernels: 66.3 us -> 63.5 us  [body(): pl.pallas_call(kernel, out_shape=jax.ShapeDtypeStruct((files, width), jnp...]
where the time goes in v6:
time: 64.5 us; the launch traced here: 64.4 us
  Pallas kernels  63.5 us (98%)
  local copies, waits for them, and re-layouts  0.88 us (1%)
    pallas_call x1, Pallas kernels, body(): pl.pallas_call(kernel, out_shape=jax.ShapeDtypeStruct((files, width), jnp...  63.5 us

profile of v6, /device:TPU:1, one launch (start us, length us, event | category | flops | bytes accessed | tf_op | source)
XLA Modules:
  0.0 64.4 jit_solution(6052503402432211493)
XLA Ops:
  0.0 63.5 %shard_map.28 = bf16[512,768]{1,0:T(8,128)(2,1)S(1)} custom-call(bf16[512,768]{1,0:T(8,128)(2,1)} %rows_hbm.1, s32[1,512]{1,0:T(1,128)} %bitcast.1), custom_call_target="tpu_custom_call" | custom-call | tf_op jit(solution)/shard_map/pallas_call | solution.py:403
  63.6 0.9 %copy.4 = bf16[512,768]{1,0:T(8,128)(2,1)} copy(bf16[512,768]{1,0:T(8,128)(2,1)S(1)} %shard_map.28) | data formatting | bytes 1572864

commit v7 on v6

--- a/solution.py
+++ b/solution.py
@@ -45,6 +45,7 @@
     raw,
     back_buf,
     home_buf,
+    match_buf,
     keys,
     key_scale,
     key_bias,
@@ -97,7 +98,6 @@
         same = (col == bucket_f) & (sub + block * 128 < lane)
         rank = rank + jnp.sum(jnp.where(same, 1.0, 0.0), axis=0, keepdims=True)
     target = bucket_f * float(SLOTS) + rank
-    slot_cols = jnp.broadcast_to(target, (128, files)).T
 
     def mixed(one, two):
         low = lax.broadcasted_iota(jnp.int32, one.shape, 1) < SLOTS
@@ -187,6 +187,23 @@
     send_slot(1, (0, 1))
     send_slot(2, (0, 1))
     send_slot(3, (1,))
+
+    number = bucket_ref[...]
+    high, mid, least = (number // place % 2 for place in (128, 16, 1))
+    flip = (high + mid + least) // 2
+    section = (
+        3 * (high + flip - 2 * high * flip)
+        + 2 * (mid + flip - 2 * mid * flip)
+        + (least + flip - 2 * least * flip)
+    )
+    chip_of = number // 32 % 4 * 16 + flip * 8 + number // 2 % 8
+    home_row = ((section * chips + chip_of) * SLOTS).astype(jnp.float32) + rank
+    slot_cols = jnp.broadcast_to(home_row, (128, files)).T
+    slot_wide = jnp.concatenate([slot_cols, slot_cols], axis=1)
+    place = lax.broadcasted_iota(jnp.int32, (files, 256), 1).astype(jnp.float32)
+    for block in range(4):
+        match = (slot_wide == place + float(block * 256)).astype(jnp.float32)
+        match_buf[block] = match.astype(jnp.bfloat16)
 
     def wait_count(buf, count, sem):
         part = buf.at[pl.ds(0, count)]
@@ -259,17 +276,15 @@
         numer[query] += summed
         denom[query] += total
 
-    def my_bucket(query):
-        offset = query + my_core * (16 + 111 * query)
-        return 32 * my_y + 2 * rem(my_hy, 8) + offset + div(my_hy, 8) * (145 - 2 * offset)
-
     def keep_back(query):
         return pltpu.make_async_copy(
-            back_buf.at[query, me], home_buf.at[my_bucket(query)], local_sem.at[4 + query]
+            back_buf.at[query, me],
+            home_buf.at[2 * my_core + query, my_y * 16 + my_hy],
+            local_sem.at[4 + query],
         )
 
     def finish(query, key):
-        mine = my_bucket(query)
+        mine = 2 * my_core + query
 
         def block_step(step, carry):
             upper = rem(div(my_y, 2) + 1 + step, 2)
@@ -289,9 +304,9 @@
                         def start_copy():
                             pltpu.make_async_remote_copy(
                                 src_ref=back_buf.at[query, to],
-                                dst_ref=home_buf.at[mine],
+                                dst_ref=home_buf.at[mine, my_y * 16 + my_hy],
                                 send_sem=send_sem.at[7 + query],
-                                recv_sem=recv_sem.at[6],
+                                recv_sem=recv_sem.at[6 + mine],
                                 device_id=(y * 2 + core, hys[column]),
                                 device_id_type=MESH,
                             ).start()
@@ -366,17 +381,19 @@
     def _():
         share(1, 4, 5).wait_send()
 
-    got = home_buf.at[pl.ds(0, BUCKETS - 2)]
-    pltpu.make_async_copy(got, got, recv_sem.at[6]).wait()
-
-    slot_wide = jnp.concatenate([slot_cols, slot_cols], axis=1)
-    place = lax.broadcasted_iota(jnp.int32, (files, 256), 1).astype(jnp.float32)
-    results = [jnp.zeros((files, half), jnp.float32) for _ in range(2)]
-    for block in range(BUCKETS * SLOTS // 256):
-        match = (slot_wide == place + float(block * 256)).astype(jnp.float32).astype(jnp.bfloat16)
-        parts = unfold_rows(home_buf[pl.ds(block * 64, 64)])
+    results = [0.0, 0.0]
+    for block in range(4):
+        for core in range(2):
+
+            @pl.when(my_core == core)
+            def _():
+                count = chips - 1 if block // 2 == core else chips
+                wait_count(home_buf.at[block], count, recv_sem.at[6 + block])
+
+        parts = unfold_rows(home_buf[block])
         results = [
-            result + jnp.dot(match, part.astype(jnp.bfloat16), preferred_element_type=jnp.float32)
+            result
+            + jnp.dot(match_buf[block], part.astype(jnp.bfloat16), preferred_element_type=jnp.float32)
             for result, part in zip(results, parts)
         ]
     out_ref[:, 0:half] = results[0].astype(jnp.bfloat16)
@@ -411,7 +428,8 @@
                 pltpu.VMEM((BUCKETS, 8, half), jnp.bfloat16),
                 pltpu.VMEM((6, devices, 8, half), jnp.bfloat16),
                 pltpu.VMEM((2, devices, 8, half), jnp.bfloat16),
-                pltpu.VMEM((BUCKETS, 8, half), jnp.bfloat16),
+                pltpu.VMEM((4, devices // 2, 8, half), jnp.bfloat16),
+                pltpu.VMEM((4, files, 256), jnp.bfloat16),
                 pltpu.VMEM((6, CAP, width), jnp.bfloat16),
                 pltpu.VMEM((6, 1, CAP), jnp.float32),
                 pltpu.VMEM((6, 1, CAP), jnp.float32),
@@ -419,7 +437,7 @@
                 pltpu.VMEM((2, CAP, width), jnp.float32),
                 pltpu.VMEM((2, CAP, 128), jnp.float32),
                 pltpu.SemaphoreType.DMA((9,)),
-                pltpu.SemaphoreType.DMA((7,)),
+                pltpu.SemaphoreType.DMA((10,)),
                 pltpu.SemaphoreType.DMA((8,)),
             ],
             compiler_params=pltpu.CompilerParams(

time: 64.5 us -> 63.7 us (0.988)
  Pallas kernels: 63.5 us -> 62.7 us
    pallas_call x1, Pallas kernels: 63.5 us -> 62.7 us  [body(): pl.pallas_call(kernel, out_shape=jax.ShapeDtypeStruct((files, width), jnp...]
where the time goes in v7:
time: 63.7 us; the launch traced here: 63.6 us
  Pallas kernels  62.7 us (98%)
  local copies, waits for them, and re-layouts  0.88 us (1%)
    pallas_call x1, Pallas kernels, body(): pl.pallas_call(kernel, out_shape=jax.ShapeDtypeStruct((files, width), jnp...  62.7 us

profile of v7, /device:TPU:1, one launch (start us, length us, event | category | flops | bytes accessed | tf_op | source)
XLA Modules:
  0.0 63.6 jit_solution(4795409115342756125)
XLA Ops:
  0.0 62.7 %shard_map.28 = bf16[512,768]{1,0:T(8,128)(2,1)S(1)} custom-call(bf16[512,768]{1,0:T(8,128)(2,1)} %rows_hbm.1, s32[1,512]{1,0:T(1,128)} %bitcast.1), custom_call_target="tpu_custom_call" | custom-call | tf_op jit(solution)/shard_map/pallas_call | solution.py:420
  62.7 0.9 %copy.4 = bf16[512,768]{1,0:T(8,128)(2,1)} copy(bf16[512,768]{1,0:T(8,128)(2,1)S(1)} %shard_map.28) | data formatting | bytes 1572864

commit v8 on v7

--- a/solution.py
+++ b/solution.py
@@ -18,6 +18,7 @@
 EMPTY = 128.0
 FAR = -1e30
 SPAN = 64
+MIXED = [at % 4 * 4 + (at // 4 + at) % 4 for at in range(16)]
 
 OFFSET = {name: 128 * (name // 100) + 16 * (name // 10 % 10) + name % 10 for name in (0, 1, 10, 11, 100, 101, 110)}
 DIRECT = ((0, 1, 101), (10, 100, 11, 110))
@@ -168,12 +169,12 @@
 
     def send_slot(slot, cores):
         def around(turn, carry):
-            ys = [rem(my_y + turn + shift, 4) for shift in range(4)]
-            for column in reversed(range(1, 16)):
+            ys = [rem(my_y + turn + 2 * my_core + shift, 4) for shift in range(4)]
+            for column in MIXED[1:]:
                 for core in cores:
                     send(ys[cross[column]], column, core, slot)
 
-            @pl.when(turn > 0)
+            @pl.when(rem(turn + 2 * my_core, 4) > 0)
             def _():
                 for core in cores:
                     send(ys[0], 0, core, slot)
@@ -297,7 +298,7 @@
 
             def give(turn, inner):
                 y = 2 * upper + rem(my_y + 1 + turn, 2)
-                for column in reversed(range(16)):
+                for column in MIXED[::-1]:
                     for core in range(2):
                         to = (y * 2 + core) * 16 + hys[column]
 

time: 63.7 us -> 62.9 us (0.987)
  Pallas kernels: 62.7 us -> 61.9 us
    pallas_call x1, Pallas kernels: 62.7 us -> 61.9 us  [body(): pl.pallas_call(kernel, out_shape=jax.ShapeDtypeStruct((files, width), jnp...]
where the time goes in v8:
time: 62.9 us; the launch traced here: 62.8 us
  Pallas kernels  61.9 us (98%)
  local copies, waits for them, and re-layouts  0.88 us (1%)
    pallas_call x1, Pallas kernels, body(): pl.pallas_call(kernel, out_shape=jax.ShapeDtypeStruct((files, width), jnp...  61.9 us

profile of v8, /device:TPU:1, one launch (start us, length us, event | category | flops | bytes accessed | tf_op | source)
XLA Modules:
  0.0 62.8 jit_solution(4062256129730151453)
XLA Ops:
  0.0 61.9 %shard_map.28 = bf16[512,768]{1,0:T(8,128)(2,1)S(1)} custom-call(bf16[512,768]{1,0:T(8,128)(2,1)} %rows_hbm.1, s32[1,512]{1,0:T(1,128)} %bitcast.1), custom_call_target="tpu_custom_call" | custom-call | tf_op jit(solution)/shard_map/pallas_call | solution.py:421
  61.9 0.9 %copy.4 = bf16[512,768]{1,0:T(8,128)(2,1)} copy(bf16[512,768]{1,0:T(8,128)(2,1)S(1)} %shard_map.28) | data formatting | bytes 1572864

commit v9 on v8

--- a/solution.py
+++ b/solution.py
@@ -297,7 +297,7 @@
             back_buf[query, pl.ds(upper * 64, 64)] = fold_rows(whole * (1.0 / under))
 
             def give(turn, inner):
-                y = 2 * upper + rem(my_y + 1 + turn, 2)
+                y = 2 * upper + rem(my_y + 1 + turn + my_core, 2)
                 for column in MIXED[::-1]:
                     for core in range(2):
                         to = (y * 2 + core) * 16 + hys[column]

time: 62.9 us -> 62.9 us (level)
  no operation moved by 1% of the time
where the time goes in v9:
time: 62.9 us; the launch traced here: 62.8 us
  Pallas kernels  61.9 us (98%)
  local copies, waits for them, and re-layouts  0.88 us (1%)
    pallas_call x1, Pallas kernels, body(): pl.pallas_call(kernel, out_shape=jax.ShapeDtypeStruct((files, width), jnp...  61.9 us

profile of v9, /device:TPU:1, one launch (start us, length us, event | category | flops | bytes accessed | tf_op | source)
XLA Modules:
  0.0 62.8 jit_solution(17349405366461971384)
XLA Ops:
  0.0 61.9 %shard_map.28 = bf16[512,768]{1,0:T(8,128)(2,1)S(1)} custom-call(bf16[512,768]{1,0:T(8,128)(2,1)} %rows_hbm.1, s32[1,512]{1,0:T(1,128)} %bitcast.1), custom_call_target="tpu_custom_call" | custom-call | tf_op jit(solution)/shard_map/pallas_call | solution.py:421
  61.9 0.9 %copy.4 = bf16[512,768]{1,0:T(8,128)(2,1)} copy(bf16[512,768]{1,0:T(8,128)(2,1)S(1)} %shard_map.28) | data formatting | bytes 1572864
